TPU v7x, 32 devices: a whole 2x2x4 slice. The times are simulated.
32 devices in a mesh: rows: 8 (over z, core), cols: 4 (over y, x).
Axes of the slice: x: 2, y: 2, z: 4, core: 2. Of those that a mesh axis runs over, the one named last changes fastest.
Arguments:
- left_factor: float32 [2048, 2048], P('rows', 'cols'), may hold values from -0.125 to 0.125
- left_cot: float32 [2048, 2048], P('rows', 'cols'), may hold values from -6 to 6
- panel_factor: float32 [2, 256, 2048], P(None, 'cols', 'rows'), may hold values from -0.125 to 0.125
- panel_cot: float32 [2, 256, 2048], P(None, 'cols', 'rows'), may hold values from -6 to 6
- rows_factor: float32 [2, 256, 2048], P(None, 'rows', 'cols'), may hold values from -0.375 to 0.375
- rows_cot: float32 [2, 256, 2048], P(None, 'rows', 'cols'), may hold values from -6 to 6
- cross_factor: float32 [256, 256], P('cols', 'rows'), may hold values from -0.375 to 0.375
- cross_cot: float32 [256, 256], P('cols', 'rows'), may hold values from -6 to 6
- diag_factor: float32 [2, 256, 256], P(None, 'rows'), as said below
- diag_cot: float32 [2, 256, 256], P(None, 'rows'), may hold values from -6 to 6
Outputs:
- left_bar: float32 [2048, 2048], P('rows', 'cols')
- rows_bar: float32 [2, 256, 2048], P(None, 'rows', 'cols')
- panel_bar: float32 [2, 256, 2048], P(None, 'cols', 'rows')
- cross_bar: float32 [256, 256], P('cols', 'rows')
- diag_bar: float32 [2, 256, 256], P(None, 'rows')
Inputs may be any that keep to these rules, and one draw needn't show every extreme that they name: `diag_factor`: each of the two blocks is lower triangular, with diagonal entries from 0.75 to 1.5; the entries below the diagonal are drawn independently with mean zero and spread at most 0.35 / sqrt(256), each of magnitude at most 1.4 / sqrt(256).
All inputs are finite; a program needn't handle non-finite values.
Results may differ from a plain program's by a relative error of at most 0.00016.
Values sent between devices are 32-bit elements; how exact they have to be, the bound alone decides.
No kernel may reach another device: no remote copies, remote signals or barrier semaphores. Data moves between devices by JAX's collectives and lax.ppermute only.
A program may use at most 64 MiB of HBM per device.

v0:
```python
import jax
import jax.numpy as jnp
from jax import lax
from jax.sharding import PartitionSpec as P

highest = lax.Precision.HIGHEST


def product(former, latter):
    return jnp.dot(former, latter, precision=highest, preferred_element_type=jnp.float32)


def halved_lower(matrix):
    return jnp.tril(matrix) - 0.5 * jnp.diag(jnp.diag(matrix))


def solve_upper(factor, values):
    return lax.linalg.triangular_solve(factor, values, left_side=True, lower=True, transpose_a=True)


def reverse_block(factor, pending):
    shaped = halved_lower(product(factor.T, pending))
    middle = solve_upper(factor, shaped)
    transposed = solve_upper(factor, middle.T)
    return transposed + transposed.T


def panel_solve(factor_cols, cot_cols, diag_whole, pending_cot):
    cot_whole = lax.all_gather(cot_cols, "cols", axis=0, tiled=True)
    solved = solve_upper(diag_whole, cot_whole)
    narrow = lax.psum(product(solved, factor_cols.T), "rows")
    partial_value = lax.all_gather(narrow, "cols", axis=1, tiled=True)
    return (solved, pending_cot - jnp.tril(partial_value))


def on_device(
    left_factor,
    left_cot,
    panel_factor,
    panel_cot,
    rows_factor,
    rows_cot,
    cross_factor,
    cross_cot,
    diag_factor,
    diag_cot,
):
    row_share = rows_factor.shape[1]
    col_share = panel_factor.shape[1]
    row_start = lax.axis_index("rows") * row_share
    col_start = lax.axis_index("cols") * col_share
    diag_whole, diag_cot_whole = (
        lax.all_gather(diag_factor, "rows", axis=1, tiled=True),
        lax.all_gather(diag_cot, "rows", axis=1, tiled=True),
    )
    upper_whole, cross_whole = (
        lax.all_gather(rows_factor[1], "rows", axis=0, tiled=True),
        lax.all_gather(cross_factor, "rows", axis=1, tiled=True),
    )
    solved_two, pending_two = panel_solve(
        panel_factor[1], panel_cot[1], diag_whole[1], diag_cot_whole[1]
    )
    left_next = left_cot - product(solved_two.T, upper_whole)
    first_cot = panel_cot[0] - product(cross_whole, solved_two)
    sym_two = reverse_block(diag_whole[1], pending_two)
    sym_rows = lax.dynamic_slice_in_dim(sym_two, row_start, row_share, 0)
    upper_local = product(solved_two, left_factor)
    cross_local = product(panel_factor[0], solved_two.T)
    upper_term, cross_term = (
        lax.psum_scatter(upper_local, "rows", scatter_dimension=0, tiled=True),
        lax.psum_scatter(cross_local, "rows", scatter_dimension=1, tiled=True),
    )
    upper_rows = rows_cot[1] - upper_term - product(sym_rows, upper_whole)
    cross_next = (
        cross_cot
        - cross_term
        - product(cross_whole, lax.dynamic_slice_in_dim(sym_two, row_start, row_share, 1))
    )
    lower_whole = lax.all_gather(rows_factor[0], "rows", axis=0, tiled=True)
    factor_cols = jnp.concatenate([cross_factor, panel_factor[0]], axis=1)
    cot_cols = jnp.concatenate([cross_next, first_cot], axis=1)
    solved_one, pending_one = panel_solve(factor_cols, cot_cols, diag_whole[0], diag_cot_whole[0])
    cross_part = solved_one[:, :row_share]
    lower_part = solved_one[:, row_share:]
    upper_rows = upper_rows - product(cross_part.T, lower_whole)
    left_next = left_next - product(lower_part.T, lower_whole)
    sym_one = reverse_block(diag_whole[0], pending_one)
    lower_local = product(cross_part, rows_factor[1]) + product(lower_part, left_factor)
    lower_term = lax.psum_scatter(lower_local, "rows", scatter_dimension=0, tiled=True)
    lower_rows = (
        rows_cot[0]
        - lower_term
        - product(lax.dynamic_slice_in_dim(sym_one, row_start, row_share, 0), lower_whole)
    )

    def own_cols(matrix):
        return lax.dynamic_slice_in_dim(matrix, col_start, col_share, 0)

    panel_out = jnp.stack([own_cols(lower_part), own_cols(solved_two)])
    cross_out = own_cols(cross_part)
    diag_out = jnp.stack(
        [
            lax.dynamic_slice_in_dim(halved_lower(sym_one), row_start, row_share, 0),
            lax.dynamic_slice_in_dim(halved_lower(sym_two), row_start, row_share, 0),
        ]
    )
    return (left_next, jnp.stack([lower_rows, upper_rows]), panel_out, cross_out, diag_out)


def solution(mesh):
    placed = (
        P("rows", "cols"),
        P("rows", "cols"),
        P(None, "cols", "rows"),
        P(None, "cols", "rows"),
        P(None, "rows", "cols"),
        P(None, "rows", "cols"),
        P("cols", "rows"),
        P("cols", "rows"),
        P(None, "rows", None),
        P(None, "rows", None),
    )
    return jax.shard_map(
        on_device,
        mesh=mesh,
        in_specs=placed,
        out_specs=(
            P("rows", "cols"),
            P(None, "rows", "cols"),
            P(None, "cols", "rows"),
            P("cols", "rows"),
            P(None, "rows", None),
        ),
        check_vma=False,
    )
```

profile of v0, /device:TPU:0, one launch (start us, length us, event | category | flops | bytes accessed | tf_op | source)
XLA Modules:
  0.0 286.8 jit_solution(2854972493506229909)
XLA Ops:
  8.2 16.5 %all_gather.27 = f32[2,256,256]{2,0,1:T(2,128)S(1)} all-gather(f32[2,32,256]{2,0,1:T(2,128)S(1)} %copy.44), channel_id=1, replica_groups=mesh['rows'=8,'cols'=4] {'rows'}, dimensions={1}, use_global_device_ids=true | all-gather | bytes 589824 | tf_op jit(solution)/shard_map/all_gather | solution.py:53
  25.2 4.0 %while.12 = (s32[]{:T(128)}, f32[256,256]{1,0:T(8,128)S(1)}, s32[2,2]{1,0:T(2,128)S(1)}, f32[2,128,128]{2,1,0:T(8,128)S(1)}, s32[]{:T(128)}) while((s32[]{:T(128)}, f32[256,256]{1,0:T(8,128)S(1)}, s32[2,2]{1,0:T(2,128)S(1)}, f32[2,128,128]{2,1,0:T(8,128)S(1)}, s32[]{:T(128)}) %tuple.71), condition=%wide.while_cond, body=%wide.while_body.sunk | while | flops 2 | bytes 131181 | solution.py:18
  29.2 19.7 %custom-call.19 = f32[2,128,128]{1,2,0:T(8,128)S(1)} custom-call(f32[2,128,128]{2,1,0:T(8,128)S(1)} %get-tuple-element.46), custom_call_target="InvertDiagBlocksLowerTriangular" | custom-call | tf_op jit(solution)/shard_map/triangular_solve/custom-call.1 | solution.py:18
  49.7 9.0 %all-gather = f32[1,256,256]{2,1,0:T(8,128)S(1)} all-gather(f32[1,64,256]{2,1,0:T(8,128)S(1)} %slice-done), channel_id=2, replica_groups=mesh['rows'=8,'cols'=4] {'cols'}, dimensions={1}, use_global_device_ids=true | all-gather | bytes 327680 | tf_op jit(solution)/shard_map/all_gather | solution.py:29
  63.2 14.1 %all_gather.32 = f32[64,256]{0,1:T(8,128)S(1)} all-gather(f32[64,32]{0,1:T(8,128)S(1)} %copy-done.12), channel_id=1, replica_groups=mesh['rows'=8,'cols'=4] {'rows'}, dimensions={1}, use_global_device_ids=true | all-gather | bytes 73728 | tf_op jit(solution)/shard_map/all_gather | solution.py:58
  77.5 14.9 %all_gather.30 = f32[2,256,256]{2,0,1:T(2,128)S(1)} all-gather(f32[2,32,256]{2,0,1:T(2,128)S(1)} %copy.48), channel_id=1, replica_groups=mesh['rows'=8,'cols'=4] {'rows'}, dimensions={1}, use_global_device_ids=true | all-gather | bytes 589824 | tf_op jit(solution)/shard_map/all_gather | solution.py:54
  94.2 4.2 %while.11 = (s32[]{:T(128)}, f32[256,256]{0,1:T(8,128)S(1)}, s32[2,2]{1,0:T(2,128)S(1)}, f32[2,128,128]{2,1,0:T(8,128)S(1)}, s32[]{:T(128)}) while((s32[]{:T(128)}, f32[256,256]{0,1:T(8,128)S(1)}, s32[2,2]{1,0:T(2,128)S(1)}, f32[2,128,128]{2,1,0:T(8,128)S(1)}, s32[]{:T(128)}) %tuple.87), condition=%wide.while_cond.1, body=%wide.while_body.1.sunk | while | flops 2 | bytes 393321 | solution.py:18
  98.5 19.7 %custom-call.6 = f32[2,128,128]{1,2,0:T(8,128)S(1)} custom-call(f32[2,128,128]{2,1,0:T(8,128)S(1)} %get-tuple-element.21), custom_call_target="InvertDiagBlocksLowerTriangular" | custom-call | tf_op jit(solution)/shard_map/triangular_solve | solution.py:18
  118.2 9.1 %all_gather.31 = f32[256,256]{0,1:T(8,128)S(1)} all-gather(f32[256,64]{0,1:T(8,128)} %all-reduce.3.cloned.1.call-done), channel_id=1, replica_groups=mesh['rows'=8,'cols'=4] {'cols'}, dimensions={1}, use_global_device_ids=true | all-gather | bytes 327680 | tf_op jit(solution)/shard_map/all_gather | solution.py:32
  127.7 2.4 gather_fusion
  132.3 16.6 %reduce-scatter.10.cloned.1.call-done = f32[32,64]{1,0:T(8,128)} async-done(((f32[256,64]{1,0:T(8,128)}), f32[32,64]{1,0:T(8,128)}) %reduce-scatter.10.cloned.1.call-update) | async-done | bytes 8208
  150.1 9.5 %all_gather.33 = f32[256,288]{1,0:T(8,128)S(1)} all-gather(f32[64,288]{1,0:T(8,128)S(1)} %pad_maximum_fusion.7), channel_id=1, replica_groups=mesh['rows'=8,'cols'=4] {'cols'}, dimensions={0}, use_global_device_ids=true | all-gather | bytes 368640 | tf_op jit(solution)/shard_map/all_gather | solution.py:29
  165.1 15.0 %all-gather.2 = f32[1,256,512]{2,1,0:T(8,128)S(1)} all-gather(f32[1,32,512]{2,1,0:T(8,128)S(1)} %get-tuple-element.137), channel_id=4, replica_groups=mesh['rows'=8,'cols'=4] {'rows'}, dimensions={1}, use_global_device_ids=true | all-gather | bytes 589824 | tf_op jit(solution)/shard_map/all_gather | solution.py:79
  180.0 15.0 %all-gather.1 = f32[1,256,512]{2,1,0:T(8,128)S(1)} all-gather(f32[1,32,512]{2,1,0:T(8,128)S(1)} %get-tuple-element.138), channel_id=3, replica_groups=mesh['rows'=8,'cols'=4] {'rows'}, dimensions={1}, use_global_device_ids=true | all-gather | bytes 589824 | tf_op jit(solution)/shard_map/all_gather | solution.py:57
  195.7 1.7 convolution_subtract_fusion.1
  197.4 2.4 gather_fusion.3
  202.1 1.4 convolution_add_fusion
  203.5 1.4 convolution_subtract_fusion
  206.4 7.9 %all-reduce.5.cloned.1.call-done = f32[256,64]{0,1:T(8,128)} async-done(((f32[256,64]{0,1:T(8,128)}), f32[256,64]{0,1:T(8,128)}) %all-reduce.5.cloned.1.call-update) | async-done | bytes 65552 | tf_op jit(solution)/shard_map/psum | solution.py:31
  214.3 9.6 %all_gather.35 = f32[256,256]{0,1:T(8,128)S(1)} all-gather(f32[256,64]{0,1:T(8,128)} %all-reduce.5.cloned.1.call-done), channel_id=1, replica_groups=mesh['rows'=8,'cols'=4] {'cols'}, dimensions={1}, use_global_device_ids=true | all-gather | bytes 327680 | tf_op jit(solution)/shard_map/all_gather | solution.py:32
  224.4 2.4 gather_fusion.1
  229.8 2.4 gather_fusion.2
  233.3 13.5 %reduce-scatter.8.cloned.1.call-done = f32[32,512]{1,0:T(8,128)} async-done(((f32[256,512]{1,0:T(8,128)}), f32[32,512]{1,0:T(8,128)}) %reduce-scatter.8.cloned.1.call-update) | async-done | bytes 65552 | tf_op jit(solution)/shard_map/reduce_scatter | solution.py:70
  248.1 30.2 %reduce-scatter.6.cloned.1.call-done = f32[32,512]{1,0:T(8,128)} async-done(((f32[256,512]{1,0:T(8,128)}), f32[32,512]{1,0:T(8,128)}) %reduce-scatter.6.cloned.1.call-update) | async-done | bytes 65552 | tf_op jit(solution)/shard_map/reduce_scatter | solution.py:89
  (134 shorter events, 38.0 us)
Async XLA Ops:
  7.2 154.8 %copy-start = (f32[256,512]{1,0:T(8,128)S(1)}, f32[256,512]{1,0:T(8,128)}, u32[]{:S(2)}) copy-start(f32[256,512]{1,0:T(8,128)} %param.12) | copy-start | bytes 1572868
  7.2 111.0 %all-reduce.3.cloned.1.call-start = ((), (), s32[]{:S(2)}) async-start(), calls=%async_computation.3 | async-start | bytes 131072 | tf_op jit(solution)/shard_map/psum | solution.py:31
  48.9 0.8 slice-start
  59.3 0.9 copy-start.6
  61.2 87.7 %reduce-scatter.10.cloned.1.call-start = ((), (), s32[]{:S(2)}) async-start(), calls=%async_computation.7 | async-start | bytes 147456
  62.5 151.9 %all-reduce.5.cloned.1.call-start = ((), (), s32[]{:S(2)}) async-start(), calls=%async_computation.5 | async-start | bytes 131072 | tf_op jit(solution)/shard_map/psum | solution.py:31
  62.5 0.7 copy-start.12
  63.2 14.2 %copy-start.13 = (f32[2,32,256]{2,1,0:T(8,128)S(1)}, f32[2,32,256]{2,1,0:T(8,128)}, u32[]{:S(2)}) copy-start(f32[2,32,256]{2,1,0:T(8,128)} %param.21) | copy-start | bytes 196612
  92.7 0.9 copy-start.7
  118.2 42.2 %copy-start.1 = (f32[2,128,128]{1,2,0:T(8,128)}, f32[2,128,128]{1,2,0:T(8,128)S(1)}, u32[]{:S(2)}) copy-start(f32[2,128,128]{1,2,0:T(8,128)S(1)} %custom-call.6) | copy-start | bytes 393220
  132.3 16.7 %copy-start.14 = (f32[64,32]{0,1:T(8,128)S(1)}, f32[64,32]{0,1:T(8,128)}, u32[]{:S(2)}) copy-start(f32[64,32]{0,1:T(8,128)} %param.19) | copy-start | bytes 24580
  161.9 84.9 %reduce-scatter.8.cloned.1.call-start = ((), (), s32[]{:S(2)}) async-start(), calls=%async_computation.6 | async-start | bytes 589824 | tf_op jit(solution)/shard_map/reduce_scatter | solution.py:70
  163.4 114.9 %reduce-scatter.6.cloned.1.call-start = ((), (), s32[]{:S(2)}) async-start(), calls=%async_computation.4 | async-start | bytes 589824 | tf_op jit(solution)/shard_map/reduce_scatter | solution.py:89
  164.2 0.9 copy-start.4
  201.1 0.9 copy-start.5
  204.9 0.8 copy-start.8
  205.8 18.2 %copy-start.3 = (f32[1,256,256]{1,2,0:T(8,128)S(1)}, f32[1,256,256]{1,2,0:T(8,128)}, u32[]{:S(2)}) copy-start(f32[1,256,256]{1,2,0:T(8,128)} %copy.76) | copy-start | bytes 786436
  226.7 0.9 copy-start.2
  229.8 2.5 copy-start.9
  229.8 2.5 copy-start.10
  232.6 14.2 %copy-start.11 = (f32[2,32,512]{2,1,0:T(8,128)S(1)}, f32[2,32,512]{2,1,0:T(8,128)}, u32[]{:S(2)}) copy-start(f32[2,32,512]{2,1,0:T(8,128)} %param.17) | copy-start | bytes 393220
Sparse Core Ops, SparseCore 0:
  61.4 55.0 all-reduce.2
  119.3 29.6 reduce-scatter.9
  162.0 52.2 all-reduce.4
  216.4 30.2 reduce-scatter.7
  248.9 29.3 reduce-scatter.5
where the time goes:
time: 288 us; the launch traced here: 287 us
  blocking collectives  113 us (39%)
  waiting for transfers between devices  68.3 us (24%)
  other arithmetic  43.3 us (15%)
  local copies, waits for them, and re-layouts  27.9 us (10%)
  matrix products  19.9 us (7%)
  between operations  14.4 us (5%)
    another operation x9, other arithmetic, solve_upper(): lax.linalg.triangular_solve(factor, values, left_side=True, lower=True, t...  39.5 us
    reduce_scatter x1, waiting for transfers between devices, on_device(): lax.psum_scatter(lower_local, 'rows', scatter_dimension=0, tiled=True)  30.2 us
    all_gather x2, blocking collectives, panel_solve(): partial_value = lax.all_gather(narrow, 'cols', axis=1, tiled=True)  18.8 us
    all_gather x2, blocking collectives, panel_solve(): cot_whole = lax.all_gather(cot_cols, 'cols', axis=0, tiled=True)  18.5 us
    unnamed x6, waiting for transfers between devices  16.7 us
    all_gather x1, blocking collectives, on_device(): lax.all_gather(diag_factor, 'rows', axis=1, tiled=True)  16.5 us
    all_gather x1, blocking collectives, on_device(): lax.all_gather(rows_factor[1], 'rows', axis=0, tiled=True)  15 us
    all_gather x1, blocking collectives, on_device(): lower_whole = lax.all_gather(rows_factor[0], 'rows', axis=0, tiled=True)  15 us
  transfers between devices with their start and end apart: 5, of which 4 were waited for; matrix products, arithmetic and copies ran while one was open for 19% of the time, Pallas kernels for 0%

commit v1 on v0

--- a/solution.py
+++ b/solution.py
@@ -4,6 +4,23 @@
 from jax.sharding import PartitionSpec as P
 
 highest = lax.Precision.HIGHEST
+
+
+def in_order(blocks, dim):
+    blocks = jnp.moveaxis(blocks, 0, dim)
+    lengths = blocks.shape
+    return blocks.reshape(*lengths[:dim], lengths[dim] * lengths[dim + 1], *lengths[dim + 2 :])
+
+
+def collected_by_bits(value, axis):
+    size, index = (lax.axis_size(axis), lax.axis_index(axis))
+    blocks, apart = (value[None], 1)
+    while apart < size:
+        theirs = lax.ppermute(blocks, axis, [(i, i ^ apart) for i in range(size)])
+        low = index & apart == 0
+        blocks = jnp.concatenate([jnp.where(low, blocks, theirs), jnp.where(low, theirs, blocks)])
+        apart *= 2
+    return blocks
 
 
 def product(former, latter):
@@ -76,7 +93,7 @@
         - cross_term
         - product(cross_whole, lax.dynamic_slice_in_dim(sym_two, row_start, row_share, 1))
     )
-    lower_whole = lax.all_gather(rows_factor[0], "rows", axis=0, tiled=True)
+    lower_whole = in_order(collected_by_bits(rows_factor[0], "rows"), 0)
     factor_cols = jnp.concatenate([cross_factor, panel_factor[0]], axis=1)
     cot_cols = jnp.concatenate([cross_next, first_cot], axis=1)
     solved_one, pending_one = panel_solve(factor_cols, cot_cols, diag_whole[0], diag_cot_whole[0])

time: 288 us -> 288 us (level)
  blocking collectives: 113 us -> 97.9 us
  waiting for transfers between devices: 68.3 us -> 79.2 us
  other arithmetic: 43.3 us -> 46.8 us
    psum x2, waiting for transfers between devices: 7.92 us -> 22.9 us  [panel_solve(): narrow = lax.psum(product(solved, factor_cols.T), 'rows')]
    all_gather x1 -> x0, blocking collectives: 15 us -> none  [on_device(): lower_whole = lax.all_gather(rows_factor[0], 'rows', axis=0, tiled=True)]
    reduce_scatter x1, waiting for transfers between devices: 13.5 us -> 0.01 us  [on_device(): lax.psum_scatter(upper_local, 'rows', scatter_dimension=0, tiled=True)]
    ppermute x0 -> x3, waiting for transfers between devices: none -> 11.7 us  [collected_by_bits(): theirs = lax.ppermute(blocks, axis, [(i, i ^ apart) for i in range(size)])]
    unnamed x37 -> x39, local copies, waits for them, and re-layouts: 7.06 us -> 5.46 us
  transfers between devices with their start and end apart: 5 -> 8, of which waited for: 4 -> 4; matrix products, arithmetic and copies ran while one was open for 19% -> 21% of each run, Pallas kernels for 0% -> 0%
where the time goes in v1:
time: 288 us; the launch traced here: 287 us
  blocking collectives  97.9 us (34%)
  waiting for transfers between devices  79.2 us (28%)
  other arithmetic  46.8 us (16%)
  local copies, waits for them, and re-layouts  27.9 us (10%)
  matrix products  18.9 us (7%)
  between operations  14.4 us (5%)
    another operation x9, other arithmetic, solve_upper(): lax.linalg.triangular_solve(factor, values, left_side=True, lower=True, t...  39.5 us
    reduce_scatter x1, waiting for transfers between devices, on_device(): lax.psum_scatter(lower_local, 'rows', scatter_dimension=0, tiled=True)  28.1 us
    psum x2, waiting for transfers between devices, panel_solve(): narrow = lax.psum(product(solved, factor_cols.T), 'rows')  22.9 us
    all_gather x2, blocking collectives, panel_solve(): partial_value = lax.all_gather(narrow, 'cols', axis=1, tiled=True)  18.6 us
    all_gather x2, blocking collectives, panel_solve(): cot_whole = lax.all_gather(cot_cols, 'cols', axis=0, tiled=True)  18.4 us
    unnamed x6, waiting for transfers between devices  16.6 us
    all_gather x1, blocking collectives, on_device(): lax.all_gather(diag_factor, 'rows', axis=1, tiled=True)  16.5 us
    all_gather x1, blocking collectives, on_device(): lax.all_gather(rows_factor[1], 'rows', axis=0, tiled=True)  15.3 us
  transfers between devices with their start and end apart: 8, of which 4 were waited for; matrix products, arithmetic and copies ran while one was open for 21% of the time, Pallas kernels for 0%

profile of v1, /device:TPU:0, one launch (start us, length us, event | category | flops | bytes accessed | tf_op | source)
XLA Modules:
  0.0 287.0 jit_solution(16999808795708452964)
XLA Ops:
  8.2 16.5 %all_gather.24 = f32[2,256,256]{2,0,1:T(2,128)S(1)} all-gather(f32[2,32,256]{2,0,1:T(2,128)S(1)} %copy.44), channel_id=1, replica_groups=mesh['rows'=8,'cols'=4] {'rows'}, dimensions={1}, use_global_device_ids=true | all-gather | bytes 589824 | tf_op jit(solution)/shard_map/all_gather | solution.py:70
  25.2 4.0 %while.12 = (s32[]{:T(128)}, f32[256,256]{1,0:T(8,128)S(1)}, s32[2,2]{1,0:T(2,128)S(1)}, f32[2,128,128]{2,1,0:T(8,128)S(1)}, s32[]{:T(128)}) while((s32[]{:T(128)}, f32[256,256]{1,0:T(8,128)S(1)}, s32[2,2]{1,0:T(2,128)S(1)}, f32[2,128,128]{2,1,0:T(8,128)S(1)}, s32[]{:T(128)}) %tuple.74), condition=%wide.while_cond, body=%wide.while_body.sunk | while | flops 2 | bytes 131181 | solution.py:35
  29.2 19.7 %custom-call.19 = f32[2,128,128]{1,2,0:T(8,128)S(1)} custom-call(f32[2,128,128]{2,1,0:T(8,128)S(1)} %get-tuple-element.46), custom_call_target="InvertDiagBlocksLowerTriangular" | custom-call | tf_op jit(solution)/shard_map/triangular_solve/custom-call.1 | solution.py:35
  49.7 9.0 %all-gather = f32[1,256,256]{2,1,0:T(8,128)S(1)} all-gather(f32[1,64,256]{2,1,0:T(8,128)S(1)} %slice-done), channel_id=2, replica_groups=mesh['rows'=8,'cols'=4] {'cols'}, dimensions={1}, use_global_device_ids=true | all-gather | bytes 327680 | tf_op jit(solution)/shard_map/all_gather | solution.py:46
  63.3 14.3 %all_gather.29 = f32[64,256]{0,1:T(8,128)S(1)} all-gather(f32[64,32]{0,1:T(8,128)S(1)} %copy-done.13), channel_id=1, replica_groups=mesh['rows'=8,'cols'=4] {'rows'}, dimensions={1}, use_global_device_ids=true | all-gather | bytes 73728 | tf_op jit(solution)/shard_map/all_gather | solution.py:75
  77.8 14.8 %all_gather.27 = f32[2,256,256]{2,0,1:T(2,128)S(1)} all-gather(f32[2,32,256]{2,0,1:T(2,128)S(1)} %copy.48), channel_id=1, replica_groups=mesh['rows'=8,'cols'=4] {'rows'}, dimensions={1}, use_global_device_ids=true | all-gather | bytes 589824 | tf_op jit(solution)/shard_map/all_gather | solution.py:71
  94.5 4.2 %while.11 = (s32[]{:T(128)}, f32[256,256]{0,1:T(8,128)S(1)}, s32[2,2]{1,0:T(2,128)S(1)}, f32[2,128,128]{2,1,0:T(8,128)S(1)}, s32[]{:T(128)}) while((s32[]{:T(128)}, f32[256,256]{0,1:T(8,128)S(1)}, s32[2,2]{1,0:T(2,128)S(1)}, f32[2,128,128]{2,1,0:T(8,128)S(1)}, s32[]{:T(128)}) %tuple.90), condition=%wide.while_cond.1, body=%wide.while_body.1.sunk | while | flops 2 | bytes 393321 | solution.py:35
  98.7 19.7 %custom-call.6 = f32[2,128,128]{1,2,0:T(8,128)S(1)} custom-call(f32[2,128,128]{2,1,0:T(8,128)S(1)} %get-tuple-element.21), custom_call_target="InvertDiagBlocksLowerTriangular" | custom-call | tf_op jit(solution)/shard_map/triangular_solve | solution.py:35
  118.4 9.1 %all_gather.28 = f32[256,256]{0,1:T(8,128)S(1)} all-gather(f32[256,64]{0,1:T(8,128)} %all-reduce.3.cloned.1.call-done), channel_id=1, replica_groups=mesh['rows'=8,'cols'=4] {'cols'}, dimensions={1}, use_global_device_ids=true | all-gather | bytes 327680 | tf_op jit(solution)/shard_map/all_gather | solution.py:49
  127.9 2.4 gather_fusion
  132.5 16.5 %reduce-scatter.10.cloned.1.call-done = f32[32,64]{1,0:T(8,128)} async-done(((f32[256,64]{1,0:T(8,128)}), f32[32,64]{1,0:T(8,128)}) %reduce-scatter.10.cloned.1.call-update) | async-done | bytes 8208
  150.1 9.5 %all_gather.30 = f32[256,288]{1,0:T(8,128)S(1)} all-gather(f32[64,288]{1,0:T(8,128)S(1)} %pad_maximum_fusion.10), channel_id=1, replica_groups=mesh['rows'=8,'cols'=4] {'cols'}, dimensions={0}, use_global_device_ids=true | all-gather | bytes 368640 | tf_op jit(solution)/shard_map/all_gather | solution.py:46
  162.0 1.4 fusion.32
  165.0 2.4 gather_fusion.3
  169.0 15.3 %all-gather.1 = f32[1,256,512]{2,1,0:T(8,128)S(1)} all-gather(f32[1,32,512]{2,1,0:T(8,128)S(1)} %get-tuple-element.143), channel_id=3, replica_groups=mesh['rows'=8,'cols'=4] {'rows'}, dimensions={1}, use_global_device_ids=true | all-gather | bytes 589824 | tf_op jit(solution)/shard_map/all_gather | solution.py:74
  188.4 1.5 convolution_add_fusion
  191.3 22.9 %all-reduce.5.cloned.1.call-done = f32[256,64]{0,1:T(8,128)} async-done(((f32[256,64]{0,1:T(8,128)}), f32[256,64]{0,1:T(8,128)}) %all-reduce.5.cloned.1.call-update) | async-done | bytes 65552 | tf_op jit(solution)/shard_map/psum | solution.py:48
  214.2 9.5 %all_gather.31 = f32[256,256]{0,1:T(8,128)S(1)} all-gather(f32[256,64]{0,1:T(8,128)} %all-reduce.5.cloned.1.call-done), channel_id=1, replica_groups=mesh['rows'=8,'cols'=4] {'cols'}, dimensions={1}, use_global_device_ids=true | all-gather | bytes 327680 | tf_op jit(solution)/shard_map/all_gather | solution.py:49
  224.1 2.4 gather_fusion.1
  228.7 2.4 gather_fusion.2
  232.1 1.5 collective-permute-start.2
  234.6 11.7 %collective-permute-done.2 = f32[4,32,512]{2,1,0:T(8,128)} collective-permute-done((f32[4,32,512]{2,1,0:T(8,128)S(1)}, f32[4,32,512]{2,1,0:T(8,128)}, u32[]{:S(2)}, u32[]{:S(2)}) %collective-permute-start.2) | collective-permute-done | bytes 262176 | tf_op jit(solution)/shard_map/ppermute | solution.py:19
  247.3 1.4 convolution_subtract_fusion
  250.5 28.1 %reduce-scatter.6.cloned.1.call-done = f32[32,512]{1,0:T(8,128)} async-done(((f32[256,512]{1,0:T(8,128)}), f32[32,512]{1,0:T(8,128)}) %reduce-scatter.6.cloned.1.call-update) | async-done | bytes 65552 | tf_op jit(solution)/shard_map/reduce_scatter | solution.py:106
  (147 shorter events, 40.9 us)
Async XLA Ops:
  7.2 154.8 %copy-start = (f32[256,512]{1,0:T(8,128)S(1)}, f32[256,512]{1,0:T(8,128)}, u32[]{:S(2)}) copy-start(f32[256,512]{1,0:T(8,128)} %param.12) | copy-start | bytes 1572868
  7.2 111.2 %all-reduce.3.cloned.1.call-start = ((), (), s32[]{:S(2)}) async-start(), calls=%async_computation.3 | async-start | bytes 131072 | tf_op jit(solution)/shard_map/psum | solution.py:48
  48.9 0.8 slice-start
  59.3 0.9 copy-start.7
  60.2 1.1 copy-start.4
  61.2 87.8 %reduce-scatter.10.cloned.1.call-start = ((), (), s32[]{:S(2)}) async-start(), calls=%async_computation.7 | async-start | bytes 147456
  61.3 106.1 %collective-permute-start = (f32[1,32,512]{2,1,0:T(8,128)S(1)}, f32[1,32,512]{2,1,0:T(8,128)}, u32[]{:S(2)}, u32[]{:S(2)}) collective-permute-start(f32[1,32,512]{2,1,0:T(8,128)S(1)} %slice.80), channel_id=1, source_target_pairs={{0,4},{4,0},{8,12},{12,8},{16,20},{20,16},{24,28},{28,24},{1,5},{5... | collective-permute-start | bytes 196616 | tf_op jit(solution)/shard_map/ppermute | solution.py:19
  62.6 151.6 %all-reduce.5.cloned.1.call-start = ((), (), s32[]{:S(2)}) async-start(), calls=%async_computation.5 | async-start | bytes 131072 | tf_op jit(solution)/shard_map/psum | solution.py:48
  62.6 0.7 copy-start.13
  63.3 14.4 %copy-start.14 = (f32[2,32,256]{2,1,0:T(8,128)S(1)}, f32[2,32,256]{2,1,0:T(8,128)}, u32[]{:S(2)}) copy-start(f32[2,32,256]{2,1,0:T(8,128)} %param.21) | copy-start | bytes 196612
  93.0 0.9 copy-start.8
  132.5 16.6 %copy-start.15 = (f32[64,32]{0,1:T(8,128)S(1)}, f32[64,32]{0,1:T(8,128)}, u32[]{:S(2)}) copy-start(f32[64,32]{0,1:T(8,128)} %param.19) | copy-start | bytes 24580
  161.9 86.9 %reduce-scatter.8.cloned.1.call-start = ((), (), s32[]{:S(2)}) async-start(), calls=%async_computation.6 | async-start | bytes 589824 | tf_op jit(solution)/shard_map/reduce_scatter | solution.py:87
  163.4 115.1 %reduce-scatter.6.cloned.1.call-start = ((), (), s32[]{:S(2)}) async-start(), calls=%async_computation.4 | async-start | bytes 589824 | tf_op jit(solution)/shard_map/reduce_scatter | solution.py:106
  165.0 2.5 copy-start.5
  168.3 16.0 %copy-start.3 = (f32[256,512]{1,0:T(8,128)S(1)}, f32[256,512]{1,0:T(8,128)}, u32[]{:S(2)}) copy-start(f32[256,512]{1,0:T(8,128)} %param.13) | copy-start | bytes 1572868
  169.0 62.1 %collective-permute-start.1 = (f32[2,32,512]{2,1,0:T(8,128)}, f32[2,32,512]{2,1,0:T(8,128)}, u32[]{:S(2)}, u32[]{:S(2)}) collective-permute-start(f32[2,32,512]{2,1,0:T(8,128)} %pad_maximum_fusion.7), channel_id=1, source_target_pairs={{0,8},{4,12},{8,0},{12,4},{16,24},{20,28},{24,16},{28,20},{1,9},{5... | collective-permute-start | bytes 393224 | tf_op jit(solution)/shard_map/ppermute | solution.py:19
  187.5 0.9 copy-start.6
  189.8 0.8 copy-start.9
  228.7 2.5 copy-start.2
  232.1 1.5 copy-start.10
  232.1 1.5 copy-start.11
  232.1 14.1 %collective-permute-start.2 = (f32[4,32,512]{2,1,0:T(8,128)S(1)}, f32[4,32,512]{2,1,0:T(8,128)}, u32[]{:S(2)}, u32[]{:S(2)}) collective-permute-start(f32[4,32,512]{2,1,0:T(8,128)S(1)} %pad_maximum_fusion.5), channel_id=1, source_target_pairs={{0,16},{4,20},{8,24},{12,28},{16,0},{20,4},{24,8},{28,12},{1,17},{... | collective-permute-start | bytes 786440 | tf_op jit(solution)/shard_map/ppermute | solution.py:19
  247.3 1.4 copy-start.12
  (1 other events, 0.7 us)
Sparse Core Ops, SparseCore 0:
  61.4 55.2 all-reduce.2
  119.5 29.5 reduce-scatter.9
  162.0 52.1 all-reduce.4
  216.3 30.6 reduce-scatter.7
  249.1 29.4 reduce-scatter.5
